TPU v7x, 32 devices: a whole 2x2x4 slice. The times are simulated.
32 devices in a mesh: grp: 2 (over x), seq: 8 (over z, y), ten: 2 (over core).
Axes of the slice: x: 2, y: 2, z: 4, core: 2. Of those that a mesh axis runs over, the one named last changes fastest.
Arguments:
- queries: bfloat16 [1024, 4096], P(('grp', 'seq'), 'ten'), parts along dimension 0, may hold values from -128 to 128
- keys: bfloat16 [1024, 512], P(('grp', 'seq'), 'ten'), parts along dimension 0, may hold values from -6 to 6
- values: bfloat16 [1024, 512], P(('grp', 'seq'), 'ten'), parts along dimension 0, may hold values from -6 to 6
- hidden: bfloat16 [1024, 8192], P(('grp', 'seq')), parts along dimension 0, may hold values from -6 to 6
- norm_gain: float32 [8192], replicated, may hold values from 0.1 to 1.9
- retained_lists: int32 [1024], P(('grp', 'seq')), parts along dimension 0, may hold values from -1 to 63, as said below
- counts: int32 [16], P('grp'), parts along dimension 0, may hold values from 0 to 64, as said below
- affine_matrix: bfloat16 [8192, 5120], P('seq', 'ten'), may hold values from -0.0625 to 0.0625
- affine_offset_vector: float32 [5120], P('ten'), may hold values from -3 to 3
Outputs:
- context: float32 [1024, 4096], P(('grp', 'seq'), 'ten'), parts along dimension 0
- col_scores: float32 [1024], P(('grp', 'seq')), parts along dimension 0
- tier_third_mapped_triples: float32 [512, 5120], P(('grp', 'seq'), 'ten'), parts along dimension 0
There are 2 independent parts, one for each index of `grp`. A program takes and returns all parts, laid end to end along the dimension named above; an argument that names none is the same for every part. Nothing has to cross between parts.
Inputs may be any that keep to these rules, and one draw needn't show every extreme that they name: `retained_lists`: entries s*64 to (s+1)*64 - 1 hold, in their first counts[s] places, the kept local rows of shard s in rising order, and -1 after them. counts sum to 256; some shard keeps all its 64 rows.
All inputs are finite; a program needn't handle non-finite values.
Results may differ from a plain program's by a relative error of at most 0.0027.
Values may be sent and summed in bfloat16 or wider, within the bound.
A program may use at most 64 MiB of HBM per device.

v0:
```python
import math
import jax
import jax.numpy as jnp
from jax import lax
from jax.sharding import PartitionSpec as P

HEAD_SIZE = 128
QUERY_HEADS = 32


def block_length(key_count):
    return math.gcd(key_count, 512)


def heads_first(queries, kv_heads):
    partition_inner_lines = queries.shape[0]
    group_width = queries.shape[1] // (HEAD_SIZE * kv_heads)
    return (
        queries.reshape(partition_inner_lines, kv_heads, group_width, HEAD_SIZE)
        .transpose(1, 2, 0, 3)
        .reshape(kv_heads, group_width * partition_inner_lines, HEAD_SIZE)
    )


def masked_scores(query_heads, query_pos, key_block, offset):
    key_count = key_block.shape[0]
    kv_heads = query_heads.shape[0]
    key_head_rows = key_block.reshape(key_count, kv_heads, HEAD_SIZE)
    scores = jnp.einsum(
        "hrd,nhd->hrn", query_heads, key_head_rows, preferred_element_type=jnp.float32
    ) * HEAD_SIZE ** (-0.5)
    key_pos = offset + jnp.arange(key_count, dtype=jnp.int32)
    allowed = key_pos[None, None, :] <= query_pos[None, :, None]
    return (scores, allowed)


def attend(carried, pieces, query_heads, query_pos):
    key_piece, value_piece = pieces
    key_count = key_piece.shape[0]
    block_rows = block_length(key_count)
    block_total = key_count // block_rows
    kv_heads = query_heads.shape[0]
    key_blocks = key_piece.reshape(block_total, block_rows, key_piece.shape[1])
    value_blocks = value_piece.reshape(block_total, block_rows, value_piece.shape[1])

    def attend_step_block(state, inputs):
        row_max, row_sum, accumulated = state
        key_block, value_block, token_count = inputs
        scores, allowed = masked_scores(query_heads, query_pos, key_block, token_count * block_rows)
        new_max = jnp.maximum(row_max, jnp.max(jnp.where(allowed, scores, -1e30), axis=2))
        weights = jnp.where(allowed, jnp.exp(scores - new_max[:, :, None]), 0.0)
        factor = jnp.exp(row_max - new_max)
        row_sum = row_sum * factor + jnp.sum(weights, axis=2)
        value_head_rows = value_block.reshape(block_rows, kv_heads, HEAD_SIZE)
        update = jnp.einsum(
            "hrn,nhd->hrd",
            weights.astype(jnp.bfloat16),
            value_head_rows,
            preferred_element_type=jnp.float32,
        )
        accumulated = accumulated * factor[:, :, None] + update
        return ((new_max, row_sum, accumulated), None)

    state, unused = lax.scan(
        attend_step_block,
        carried,
        (key_blocks, value_blocks, jnp.arange(block_total, dtype=jnp.int32)),
    )
    return state


def column_terms(key_piece, query_heads, query_pos, log_total):
    key_count = key_piece.shape[0]
    block_rows = block_length(key_count)
    block_total = key_count // block_rows
    key_blocks = key_piece.reshape(block_total, block_rows, key_piece.shape[1])

    def column_step_block(state, inputs):
        key_block, token_count = inputs
        scores, allowed = masked_scores(query_heads, query_pos, key_block, token_count * block_rows)
        weights = jnp.where(allowed, jnp.exp(scores - log_total[:, :, None]), 0.0)
        return (state, jnp.sum(weights, axis=(0, 1)))

    unused, sums = lax.scan(
        column_step_block, jnp.float32(0.0), (key_blocks, jnp.arange(block_total, dtype=jnp.int32))
    )
    return sums.reshape(key_count)


def shards(
    queries,
    keys,
    values,
    hidden,
    norm_gain,
    retained_lists,
    counts,
    affine_matrix,
    affine_offset_vector,
):
    partition_inner_lines = queries.shape[0]
    kv_heads = keys.shape[1] // HEAD_SIZE
    group_width = queries.shape[1] // keys.shape[1]
    seq_index = lax.axis_index("seq")
    query_heads = heads_first(queries, kv_heads)
    query_pos = seq_index * partition_inner_lines + jnp.tile(
        jnp.arange(partition_inner_lines, dtype=jnp.int32), group_width
    )
    packed_rows = group_width * partition_inner_lines
    initial = (
        jnp.full((kv_heads, packed_rows), -1e30, jnp.float32),
        jnp.zeros((kv_heads, packed_rows), jnp.float32),
        jnp.zeros((kv_heads, packed_rows, HEAD_SIZE), jnp.float32),
    )
    row_max, row_sum, accumulated = attend(
        initial,
        (
            lax.all_gather(keys, "seq", axis=0, tiled=True),
            lax.all_gather(values, "seq", axis=0, tiled=True),
        ),
        query_heads,
        query_pos,
    )
    log_total = row_max + jnp.log(row_sum)
    column_part = column_terms(
        lax.all_gather(keys, "seq", axis=0, tiled=True), query_heads, query_pos, log_total
    )
    context = (
        (accumulated / row_sum[:, :, None])
        .reshape(kv_heads, group_width, partition_inner_lines, HEAD_SIZE)
        .transpose(2, 0, 1, 3)
        .reshape(partition_inner_lines, queries.shape[1])
    )
    column_rows = lax.psum_scatter(column_part, "seq", scatter_dimension=0, tiled=True)
    col_scores = lax.psum(column_rows, "ten") / QUERY_HEADS
    hidden_f = hidden.astype(jnp.float32)
    rescaled_activations = (
        hidden_f
        * lax.rsqrt(jnp.mean(hidden_f * hidden_f, axis=1, keepdims=True) + 1e-06)
        * norm_gain
    ).astype(jnp.bfloat16)
    selector = (
        retained_lists[:, None] == jnp.arange(partition_inner_lines, dtype=jnp.int32)[None, :]
    ).astype(jnp.bfloat16)
    chosen = jnp.dot(selector, rescaled_activations, preferred_element_type=jnp.float32).astype(
        jnp.bfloat16
    )
    sequence_total = lax.axis_size("seq")
    retained_total = sequence_total * partition_inner_lines // 2
    retained_element = jnp.arange(retained_total, dtype=jnp.int32)
    partition_finish_marks = jnp.cumsum(counts)
    holder_partition = jnp.sum(
        (partition_finish_marks[None, :] <= retained_element[:, None]).astype(jnp.int32), axis=1
    )
    starts = partition_finish_marks - counts
    opening_marks = jnp.sum(
        jnp.where(
            jnp.arange(sequence_total, dtype=jnp.int32)[None, :] == holder_partition[:, None],
            starts[None, :],
            0,
        ),
        axis=1,
    )
    retained_place_number = retained_element - opening_marks
    received = lax.all_to_all(chosen, "seq", split_axis=1, concat_axis=0, tiled=True)
    provenance = holder_partition * partition_inner_lines + retained_place_number
    compact = jnp.take(received, provenance, axis=0)
    projected = lax.psum_scatter(
        jnp.dot(compact, affine_matrix, preferred_element_type=jnp.float32),
        "seq",
        scatter_dimension=0,
        tiled=True,
    )
    tier_third_mapped_triples = projected + affine_offset_vector
    return (context, col_scores, tier_third_mapped_triples)


def solution(mesh):
    in_specs = (
        P(("grp", "seq"), "ten"),
        P(("grp", "seq"), "ten"),
        P(("grp", "seq"), "ten"),
        P(("grp", "seq"), None),
        P(),
        P(("grp", "seq")),
        P("grp"),
        P("seq", "ten"),
        P("ten"),
    )
    out_specs = (P(("grp", "seq"), "ten"), P(("grp", "seq")), P(("grp", "seq"), "ten"))
    return jax.shard_map(shards, mesh=mesh, in_specs=in_specs, out_specs=out_specs, check_vma=False)
```

profile of v0, /device:TPU:0, one launch (start us, length us, event | category | flops | bytes accessed | tf_op | source)
XLA Modules:
  0.0 152.0 jit_solution(15588536419003187684)
XLA Ops:
  7.2 1.5 %fusion = f32[64]{0:T(128)S(1)} fusion(bf16[64,8192]{1,0:T(8,128)(2,1)} %param.12), kind=kLoop, calls=%fused_computation.4 | loop fusion | flops 1572800 | bytes 1048832 | tf_op jit(solution)/shard_map/reduce_sum | solution.py:139
  8.7 1.7 %convolution_convert_fusion = bf16[64,8192]{1,0:T(8,128)(2,1)S(1)} fusion(bf16[64,8192]{1,0:T(8,128)(2,1)} %param.12, f32[8192]{0:T(1024)} %param.13, f32[64]{0:T(128)S(1)} %add_rsqrt_fusion, s32[64]{0:T(128)} %param.14), kind=kOutput, calls=%fused_computation.1 | convolution fusion | flops 69734400 | bytes 2130432 | tf_op jit(solution)/shard_map/dot_general | solution.py:145
  10.5 0.0 copy-start.4
  10.5 1.1 copy.48
  11.6 7.3 %all-to-all-start = ((bf16[64,8,1024]{2,0,1:T(8,128)(2,1)}), bf16[64,8,1024]{2,0,1:T(8,128)(2,1)S(1)}, u32[]{:S(2)}, u32[]{:S(2)}) async-start(bf16[64,8,1024]{2,0,1:T(8,128)(2,1)} %bitcast.32), calls=%async_computation | async-start | bytes 2097152 | tf_op jit(solution)/shard_map/all_to_all | solution.py:165
  18.9 0.0 reduce-scatter.2.cloned.1.call-start
  18.9 0.0 copy-done.4
  18.9 0.2 reduce-window.8
  19.1 0.1 convert_reduce_fusion
  19.2 0.1 select_reduce_fusion.2
  19.3 25.3 %all-to-all-done = bf16[64,8,1024]{2,0,1:T(8,128)(2,1)S(1)} async-done(((bf16[64,8,1024]{2,0,1:T(8,128)(2,1)}), bf16[64,8,1024]{2,0,1:T(8,128)(2,1)S(1)}, u32[]{:S(2)}, u32[]{:S(2)}) %all-to-all-start) | async-done | bytes 1048608 | tf_op jit(solution)/shard_map/all_to_all | solution.py:165
  44.6 1.2 gather_fusion
  45.8 5.6 %fusion.14 = f32[256,2560]{1,0:T(8,128)} fusion(bf16[1024,2560]{1,0:T(8,128)(2,1)} %param.16, bf16[256,1024]{1,0:T(8,128)(2,1)S(1)} %gather_fusion, pred[256]{0:T(512)(128)(4,1)S(1)} %compare_and_fusion), kind=kOutput, calls=%fused_computation.23 | convolution fusion | flops 1342439424 | bytes 8388864 | tf_op jit(solution)/shard_map/dot_general | solution.py:169
  51.4 0.0 copy-start
  51.4 0.0 copy-start.1
  51.4 0.0 copy-start.2
  51.4 0.0 reduce-scatter.2.cloned.1.call-update
  51.4 0.1 add.110
  51.5 0.8 copy-done
  52.4 0.1 copy.32
  52.4 0.0 copy-done.1
  52.4 31.7 %all_gather.7 = bf16[512,256]{1,0:T(8,128)(2,1)S(1)} all-gather(bf16[64,256]{1,0:T(8,128)(2,1)S(1)} %copy-done.1), channel_id=1, replica_groups=mesh['grp'=2,'seq'=8,'ten'=2] {'seq'}, dimensions={0}, use_global_device_ids=true | all-gather | bytes 294912 | tf_op jit(solution)/shard_map/all_gather | solution.py:118
  84.2 0.1 copy.33
  84.3 0.0 copy-done.2
  84.3 31.4 %all_gather.8 = bf16[512,256]{1,0:T(8,128)(2,1)S(1)} all-gather(bf16[64,256]{1,0:T(8,128)(2,1)S(1)} %copy-done.2), channel_id=1, replica_groups=mesh['grp'=2,'seq'=8,'ten'=2] {'seq'}, dimensions={0}, use_global_device_ids=true | all-gather | bytes 294912 | tf_op jit(solution)/shard_map/all_gather | solution.py:119
  115.7 0.1 copy.35
  115.9 0.2 iota_compare_fusion
  116.0 0.6 select_reduce_fusion.1
  116.7 0.5 fusion.3
  117.2 0.9 fusion.5
  118.2 0.0 copy-start.5
  118.2 0.0 copy-start.3
  118.2 0.3 copy.38
  118.5 1.0 copy.49
  119.5 0.0 copy-done.5
  119.5 0.6 dynamic-slice.2
  120.7 0.6 select_reduce_fusion
  121.3 19.1 %all-reduce = f32[512]{0:T(512)S(1)} all-reduce(f32[512]{0:T(512)S(1)} %select_reduce_fusion), channel_id=2, replica_groups=mesh['grp'=2,'seq'=8,'ten'=2] {'seq'}, use_global_device_ids=true, to_apply=%region_3.4.clone | all-reduce | flops 512 | bytes 4096
  140.4 0.1 dynamic-slice.3
  140.4 2.4 %psum.7 = f32[64]{0:T(128)S(1)} all-reduce(f32[64]{0:T(128)S(1)} %dynamic-slice.3), channel_id=1, replica_groups=mesh['grp'=2,'seq'=8,'ten'=2] {'ten'}, use_global_device_ids=true, to_apply=%region_4.5 | all-reduce | flops 64 | bytes 512 | tf_op jit(solution)/shard_map/psum | solution.py:135
  142.9 0.5 broadcast_multiply_fusion.1
  143.4 0.0 reduce-scatter.2.cloned.1.call-done
  143.4 0.0 copy-done.3
  143.4 1.7 %broadcast_add_fusion = f32[32,2560]{1,0:T(8,128)} fusion(f32[32,2560]{1,0:T(8,128)} %reduce-scatter.2.cloned.1.call-done, f32[2560]{0:T(1024)S(1)} %copy-done.3), kind=kLoop, calls=%fused_computation.27 | loop fusion | flops 81920 | bytes 665600 | tf_op jit(solution)/shard_map/add | solution.py:174
  (10 shorter events, 0.1 us)
Async XLA Ops:
  10.5 8.5 %copy-start.4 = (s32[8]{0:T(128)S(1)}, s32[8]{0:T(128)}, u32[]{:S(2)}) copy-start(s32[8]{0:T(128)} %param.15) | copy-start | bytes 100
  11.6 33.1 %all-to-all-start = ((bf16[64,8,1024]{2,0,1:T(8,128)(2,1)}), bf16[64,8,1024]{2,0,1:T(8,128)(2,1)S(1)}, u32[]{:S(2)}, u32[]{:S(2)}) async-start(bf16[64,8,1024]{2,0,1:T(8,128)(2,1)} %bitcast.32), calls=%async_computation | async-start | bytes 2097152 | tf_op jit(solution)/shard_map/all_to_all | solution.py:165
  18.9 124.5 %reduce-scatter.2.cloned.1.call-start = ((), (), s32[]{:S(2)}) async-start(), calls=%async_computation.2 | async-start | bytes 2949120 | tf_op jit(solution)/shard_map/reduce_scatter | solution.py:168
  51.4 0.9 copy-start
  51.4 1.1 copy-start.1
  51.4 32.9 %copy-start.2 = (bf16[64,256]{1,0:T(8,128)(2,1)S(1)}, bf16[64,256]{1,0:T(8,128)(2,1)}, u32[]{:S(2)}) copy-start(bf16[64,256]{1,0:T(8,128)(2,1)} %param.11) | copy-start | bytes 98308
  118.2 1.3 copy-start.5
  118.2 25.2 %copy-start.3 = (f32[2560]{0:T(1024)S(1)}, f32[2560]{0:T(1024)}, u32[]{:S(2)}) copy-start(f32[2560]{0:T(1024)} %param.17) | copy-start | bytes 30724
Sparse Core Ops, SparseCore 0:
  51.5 72.2 reduce-scatter.1
where the time goes:
time: 152 us
  blocking collectives  84.7 us (56%)
  waiting for transfers between devices  25.3 us (17%)
  between operations  14.8 us (10%)
  matrix products  8.9 us (6%)
  starting transfers between devices  7.35 us (5%)
  local copies, waits for them, and re-layouts  5.49 us (4%)
  other arithmetic  5.4 us (4%)
    all_gather x1, blocking collectives, shards(): lax.all_gather(keys, 'seq', axis=0, tiled=True)  31.7 us
    all_gather x1, blocking collectives, shards(): lax.all_gather(values, 'seq', axis=0, tiled=True)  31.4 us
    all_to_all x1, waiting for transfers between devices, shards(): lax.all_to_all(chosen, 'seq', split_axis=1, concat_axis=0, tiled=True)  25.3 us
    unnamed x1, blocking collectives  19.1 us
    all_to_all x1, starting transfers between devices, shards(): lax.all_to_all(chosen, 'seq', split_axis=1, concat_axis=0, tiled=True)  7.31 us
    dot_general x1, matrix products, shards(): jnp.dot(compact, affine_matrix, preferred_element_type=jnp.float32)  5.57 us
  transfers between devices with their start and end apart: 2, of which 1 were waited for; matrix products, arithmetic and copies ran while one was open for 4% of the time, Pallas kernels for 0%

commit v1 on v0

--- a/solution.py
+++ b/solution.py
@@ -1,3 +1,4 @@
+import functools
 import math
 import jax
 import jax.numpy as jnp
@@ -6,6 +7,16 @@
 
 HEAD_SIZE = 128
 QUERY_HEADS = 32
+
+
+def change_meshes_by_axis(x_local, device_axis):
+    fresh = jnp.split(x_local, lax.axis_size(device_axis), axis=1)
+    e_next = jnp.stack(fresh)
+    z = lax.all_to_all(e_next, device_axis, 0, 0)
+    return jnp.concatenate(z, axis=0)
+
+
+lay_slot = functools.partial(change_meshes_by_axis, device_axis="seq")
 
 
 def block_length(key_count):
@@ -162,7 +173,7 @@
         axis=1,
     )
     retained_place_number = retained_element - opening_marks
-    received = lax.all_to_all(chosen, "seq", split_axis=1, concat_axis=0, tiled=True)
+    received = lay_slot(chosen)
     provenance = holder_partition * partition_inner_lines + retained_place_number
     compact = jnp.take(received, provenance, axis=0)
     projected = lax.psum_scatter(

time: 152 us -> 156 us (1.026)
  local copies, waits for them, and re-layouts: 5.49 us -> 9.57 us
    unnamed x16 -> x23, local copies, waits for them, and re-layouts: 2.5 us -> 6.99 us
where the time goes in v1:
time: 156 us
  blocking collectives  84.6 us (54%)
  waiting for transfers between devices  25.3 us (16%)
  between operations  14.9 us (10%)
  local copies, waits for them, and re-layouts  9.57 us (6%)
  matrix products  8.91 us (6%)
  starting transfers between devices  7.35 us (5%)
  other arithmetic  5.4 us (3%)
    all_gather x1, blocking collectives, shards(): lax.all_gather(values, 'seq', axis=0, tiled=True)  31.9 us
    all_gather x1, blocking collectives, shards(): lax.all_gather(keys, 'seq', axis=0, tiled=True)  31.5 us
    all_to_all x1, waiting for transfers between devices, change_meshes_by_axis(): z = lax.all_to_all(e_next, device_axis, 0, 0)  25.3 us
    unnamed x1, blocking collectives  18.8 us
    all_to_all x1, starting transfers between devices, change_meshes_by_axis(): z = lax.all_to_all(e_next, device_axis, 0, 0)  7.31 us
    unnamed x23, local copies, waits for them, and re-layouts  6.99 us
    dot_general x1, matrix products, shards(): jnp.dot(compact, affine_matrix, preferred_element_type=jnp.float32)  5.56 us
  transfers between devices with their start and end apart: 2, of which 1 were waited for; matrix products, arithmetic and copies ran while one was open for 4% of the time, Pallas kernels for 0%

profile of v1, /device:TPU:0, one launch (start us, length us, event | category | flops | bytes accessed | tf_op | source)
XLA Modules:
  0.0 156.0 jit_solution(15554792290841420468)
XLA Ops:
  7.2 1.5 fusion
  8.7 1.7 %convolution_convert_fusion = bf16[64,8192]{1,0:T(8,128)(2,1)S(1)} fusion(bf16[64,8192]{1,0:T(8,128)(2,1)} %param.12, f32[8192]{0:T(1024)} %param.13, f32[64]{0:T(128)S(1)} %add_rsqrt_fusion, s32[64]{0:T(128)} %param.14), kind=kOutput, calls=%fused_computation.1 | convolution fusion | flops 69734400 | bytes 2130432 | tf_op jit(solution)/shard_map/dot_general | solution.py:156
  10.5 0.0 copy-start.4
  10.5 0.6 fusion.25
  11.1 0.7 fusion.24
  11.8 0.7 fusion.23
  12.5 0.7 fusion.22
  13.1 0.7 fusion.21
  13.8 0.6 fusion.20
  14.4 0.7 fusion.19
  15.1 0.7 fusion.18
  15.7 7.3 %all-to-all-start = ((bf16[8,64,1024]{2,1,0:T(8,128)(2,1)}), bf16[8,64,1024]{2,1,0:T(8,128)(2,1)S(1)}, u32[]{:S(2)}, u32[]{:S(2)}) async-start(bf16[8,64,1024]{2,1,0:T(8,128)(2,1)} %fusion.18), calls=%async_computation | async-start | bytes 2097152 | tf_op jit(solution)/shard_map/all_to_all | solution.py:15
  23.1 0.0 reduce-scatter.2.cloned.1.call-start
  23.1 0.0 copy-done.4
  23.1 0.2 reduce-window.8
  23.3 0.1 convert_reduce_fusion
  23.4 0.1 select_reduce_fusion.2
  23.5 25.3 %all-to-all-done = bf16[8,64,1024]{2,1,0:T(8,128)(2,1)S(1)} async-done(((bf16[8,64,1024]{2,1,0:T(8,128)(2,1)}), bf16[8,64,1024]{2,1,0:T(8,128)(2,1)S(1)}, u32[]{:S(2)}, u32[]{:S(2)}) %all-to-all-start) | async-done | bytes 1048608 | tf_op jit(solution)/shard_map/all_to_all | solution.py:15
  48.8 1.2 gather_fusion
  50.0 5.6 %fusion.14 = f32[256,2560]{1,0:T(8,128)} fusion(bf16[1024,2560]{1,0:T(8,128)(2,1)} %param.16, bf16[256,1024]{1,0:T(8,128)(2,1)S(1)} %gather_fusion, pred[256]{0:T(512)(128)(4,1)S(1)} %compare_and_fusion), kind=kOutput, calls=%fused_computation.22 | convolution fusion | flops 1342439424 | bytes 8388864 | tf_op jit(solution)/shard_map/dot_general | solution.py:180
  55.6 0.0 copy-start.1
  55.6 0.0 reduce-scatter.2.cloned.1.call-update
  55.6 0.7 copy-done.1
  56.3 31.9 %all_gather.8 = bf16[512,256]{1,0:T(8,128)(2,1)S(1)} all-gather(bf16[64,256]{1,0:T(8,128)(2,1)S(1)} %copy-done.1), channel_id=1, replica_groups=mesh['grp'=2,'seq'=8,'ten'=2] {'seq'}, dimensions={0}, use_global_device_ids=true | all-gather | bytes 294912 | tf_op jit(solution)/shard_map/all_gather | solution.py:130
  88.2 0.1 copy.32
  88.4 0.1 add.110
  88.4 0.0 copy-done
  88.5 0.1 copy.29
  88.6 0.0 copy-done.2
  88.6 31.5 %all_gather.7 = bf16[512,256]{1,0:T(8,128)(2,1)S(1)} all-gather(bf16[64,256]{1,0:T(8,128)(2,1)S(1)} %copy-done.2), channel_id=1, replica_groups=mesh['grp'=2,'seq'=8,'ten'=2] {'seq'}, dimensions={0}, use_global_device_ids=true | all-gather | bytes 294912 | tf_op jit(solution)/shard_map/all_gather | solution.py:129
  120.1 0.1 copy.30
  120.2 0.2 iota_compare_fusion
  120.4 0.6 select_reduce_fusion.1
  121.1 0.5 fusion.3
  121.6 1.0 fusion.5
  122.5 0.0 copy-start.5
  122.6 0.0 copy-start.3
  122.6 0.3 copy.35
  122.9 1.0 copy.42
  123.8 0.0 copy-done.5
  123.8 0.6 dynamic-slice.2
  125.1 0.6 select_reduce_fusion
  125.6 18.8 %all-reduce = f32[512]{0:T(512)S(1)} all-reduce(f32[512]{0:T(512)S(1)} %select_reduce_fusion), channel_id=2, replica_groups=mesh['grp'=2,'seq'=8,'ten'=2] {'seq'}, use_global_device_ids=true, to_apply=%region_3.4.clone | all-reduce | flops 512 | bytes 4096
  144.4 0.1 dynamic-slice.3
  144.5 2.4 %psum.7 = f32[64]{0:T(128)S(1)} all-reduce(f32[64]{0:T(128)S(1)} %dynamic-slice.3), channel_id=1, replica_groups=mesh['grp'=2,'seq'=8,'ten'=2] {'ten'}, use_global_device_ids=true, to_apply=%region_4.5 | all-reduce | flops 64 | bytes 512 | tf_op jit(solution)/shard_map/psum | solution.py:146
  147.0 0.5 broadcast_multiply_fusion.1
  147.5 0.0 copy-done.3
  147.5 1.7 %broadcast_add_fusion = f32[32,2560]{1,0:T(8,128)} fusion(f32[32,2560]{1,0:T(8,128)} %reduce-scatter.2.cloned.1.call-done, f32[2560]{0:T(1024)S(1)} %copy-done.3), kind=kLoop, calls=%fused_computation.26 | loop fusion | flops 81920 | bytes 665600 | tf_op jit(solution)/shard_map/add | solution.py:185
  (13 shorter events, 0.1 us)
Async XLA Ops:
  10.5 12.6 %copy-start.4 = (s32[8]{0:T(128)S(1)}, s32[8]{0:T(128)}, u32[]{:S(2)}) copy-start(s32[8]{0:T(128)} %param.15) | copy-start | bytes 100
  15.7 33.1 %all-to-all-start = ((bf16[8,64,1024]{2,1,0:T(8,128)(2,1)}), bf16[8,64,1024]{2,1,0:T(8,128)(2,1)S(1)}, u32[]{:S(2)}, u32[]{:S(2)}) async-start(bf16[8,64,1024]{2,1,0:T(8,128)(2,1)} %fusion.18), calls=%async_computation | async-start | bytes 2097152 | tf_op jit(solution)/shard_map/all_to_all | solution.py:15
  23.1 124.4 %reduce-scatter.2.cloned.1.call-start = ((), (), s32[]{:S(2)}) async-start(), calls=%async_computation.2 | async-start | bytes 2949120 | tf_op jit(solution)/shard_map/reduce_scatter | solution.py:179
  55.6 0.8 copy-start.1
  55.6 32.9 %copy-start = (bf16[64,2048]{1,0:T(8,128)(2,1)S(1)}, bf16[64,2048]{1,0:T(8,128)(2,1)}, u32[]{:S(2)}) copy-start(bf16[64,2048]{1,0:T(8,128)(2,1)} %param.9) | copy-start | bytes 786436
  55.6 33.0 %copy-start.2 = (bf16[64,256]{1,0:T(8,128)(2,1)S(1)}, bf16[64,256]{1,0:T(8,128)(2,1)}, u32[]{:S(2)}) copy-start(bf16[64,256]{1,0:T(8,128)(2,1)} %param.10) | copy-start | bytes 98308
  122.5 1.3 copy-start.5
  122.6 24.9 %copy-start.3 = (f32[2560]{0:T(1024)S(1)}, f32[2560]{0:T(1024)}, u32[]{:S(2)}) copy-start(f32[2560]{0:T(1024)} %param.17) | copy-start | bytes 30724
Sparse Core Ops, SparseCore 0:
  55.7 71.7 reduce-scatter.1
